TPU v7x, 32 devices: a whole 2x2x4 slice. The times are simulated.
32 devices in a mesh: dp: 4 (over y, x), fsdp: 8 (over z, core).
Axes of the slice: x: 2, y: 2, z: 4, core: 2. Of those that a mesh axis runs over, the one named last changes fastest.
Arguments:
- tokens_in: bfloat16 [32, 256, 1024], P(('dp', 'fsdp')), may hold values from -6 to 6
- cotangent: bfloat16 [32, 256, 1024], P(('dp', 'fsdp')), may hold values from -6 to 6
- lengths: int32 [32], P(('dp', 'fsdp')), may hold values from 128 to 256
- qkv_master: float32 [1024, 3072], P('fsdp'), may hold values from -0.5625 to 0.5625
- out_master: float32 [1024, 1024], P('fsdp'), may hold values from -2.25 to 2.25
- up_master: float32 [1024, 4096], P('fsdp'), may hold values from -0.5625 to 0.5625
- down_master: float32 [4096, 1024], P('fsdp'), may hold values from -0.28125 to 0.28125
- small_master: float32 [13312], P('fsdp'), may hold values from -0.8 to 1.4
- qkv_first: float32 [1024, 3072], P('fsdp'), may hold values from -814.58701 to 814.58701
- out_first: float32 [1024, 1024], P('fsdp'), may hold values from -407.29351 to 407.29351
- up_first: float32 [1024, 4096], P('fsdp'), may hold values from -814.58701 to 814.58701
- down_first: float32 [4096, 1024], P('fsdp'), may hold values from -814.58701 to 814.58701
- small_first: float32 [13312], P('fsdp'), may hold values from -1629.17402 to 1629.17402
- qkv_second: float32 [1024, 3072], P('fsdp'), may hold values from 2048 to 8192
- out_second: float32 [1024, 1024], P('fsdp'), may hold values from 512 to 2048
- up_second: float32 [1024, 4096], P('fsdp'), may hold values from 2048 to 8192
- down_second: float32 [4096, 1024], P('fsdp'), may hold values from 2048 to 8192
- small_second: float32 [13312], P('fsdp'), may hold values from 8192 to 32768
Outputs:
- output: bfloat16 [32, 256, 1024], P(('dp', 'fsdp'))
- input_grad: bfloat16 [32, 256, 1024], P(('dp', 'fsdp'))
- qkv_new: float32 [1024, 3072], P('fsdp')
- out_new: float32 [1024, 1024], P('fsdp')
- up_new: float32 [1024, 4096], P('fsdp')
- down_new: float32 [4096, 1024], P('fsdp')
- small_new: float32 [13312], P('fsdp')
- qkv_first_new: float32 [1024, 3072], P('fsdp')
- out_first_new: float32 [1024, 1024], P('fsdp')
- up_first_new: float32 [1024, 4096], P('fsdp')
- down_first_new: float32 [4096, 1024], P('fsdp')
- small_first_new: float32 [13312], P('fsdp')
- qkv_second_new: float32 [1024, 3072], P('fsdp')
- out_second_new: float32 [1024, 1024], P('fsdp')
- up_second_new: float32 [1024, 4096], P('fsdp')
- down_second_new: float32 [4096, 1024], P('fsdp')
- small_second_new: float32 [13312], P('fsdp')
- lamb_norms: float32 [2, 5], replicated
All inputs are finite; a program needn't handle non-finite values.
Results may differ from a plain program's by a relative error of at most 0.012.
The roundings to bfloat16 on the way count: a program that leaves them out, or rounds other values in their place, can miss the bound.
Values may be sent and summed in bfloat16 or wider, within the bound.
A program may use at most 256 MiB of HBM per device.

v0:
```python
import math
import jax
import jax.numpy as jnp
from jax import lax
from jax.sharding import PartitionSpec as P

D = 1024
HEADS = 16
HD = 64
FF = 4096
ROT = 16
NORM_EPSILON = 1e-05
ADAM_EPSILON = 1e-06
ROPE_BASE = 10000.0
RATE = 0.5
DECAY = 0.01
BETA_ONE = 0.5
BETA_TWO = 0.5


def split_small(small_vector):
    bounds = [0, D, 2 * D, 3 * D, 4 * D, 7 * D, 8 * D, 8 * D + FF, 9 * D + FF]
    return [small_vector[bounds[number] : bounds[number + 1]] for number in range(8)]


def normalize(values):
    average = jnp.mean(values, axis=-1, keepdims=True)
    centred = values - average
    variance = jnp.mean(centred * centred, axis=-1, keepdims=True)
    inverse = lax.rsqrt(variance + NORM_EPSILON)
    return (centred * inverse, inverse)


def rotary_tables(length):
    half_dims = ROT // 2
    position = jnp.arange(length, dtype=jnp.float32)[:, None]
    number = jnp.arange(half_dims, dtype=jnp.float32)[None, :]
    angle = position * jnp.exp(number * (-2.0 * math.log(ROPE_BASE) / ROT))
    return (jnp.cos(angle)[:, None, :], jnp.sin(angle)[:, None, :])


def rotate(heads_in, cosine_table, sine_table):
    half_dims = ROT // 2
    first_half = heads_in[..., :half_dims]
    second_half = heads_in[..., half_dims:ROT]
    return jnp.concatenate(
        [
            first_half * cosine_table - second_half * sine_table,
            second_half * cosine_table + first_half * sine_table,
            heads_in[..., ROT:],
        ],
        axis=-1,
    )


def rotate_back(grads_in, cosine_table, sine_table):
    half_dims = ROT // 2
    first_half = grads_in[..., :half_dims]
    second_half = grads_in[..., half_dims:ROT]
    return jnp.concatenate(
        [
            first_half * cosine_table + second_half * sine_table,
            second_half * cosine_table - first_half * sine_table,
            grads_in[..., ROT:],
        ],
        axis=-1,
    )


def gelu_slope(values):
    return 0.5 * (1.0 + lax.erf(values * 2.0 ** (-0.5))) + values * jnp.exp(
        -0.5 * values * values
    ) * (2.0 * math.pi) ** (-0.5)


def against(left, right):
    return lax.dot_general(
        left, right, (((1,), (1,)), ((), ())), preferred_element_type=jnp.float32
    )


def outer_sum(columns, right):
    return lax.dot_general(
        columns, right, (((0,), (0,)), ((), ())), preferred_element_type=jnp.float32
    )


def local_squares(arrays):
    return jnp.stack([jnp.sum(array_in * array_in) for array_in in arrays])


def sliced(master, part, parts, pieces):
    rows, columns = master.shape
    width = columns // (pieces * parts)
    return lax.dynamic_index_in_dim(
        master.reshape(rows, pieces, parts, width), part, axis=2, keepdims=False
    ).reshape(rows, pieces * width)


def joined(slices, pieces):
    parts, rows, columns = slices.shape
    width = columns // pieces
    return (
        slices.reshape(parts, rows, pieces, width)
        .transpose(1, 2, 0, 3)
        .reshape(rows, pieces * parts * width)
    )


def layer(x_all, cotangent_all, lengths_all, weights, small_all, part):
    qkv_weight, out_weight, up_weight, down_weight = weights
    group, length, _ = x_all.shape
    tokens = group * length
    head_cols = out_weight.shape[0]
    heads = head_cols // HD
    gain_one, shift_one, gain_two, shift_two, qkv_bias, up_bias = small_all
    inputs = x_all.reshape(tokens, D).astype(jnp.float32)
    position = jnp.arange(length)
    live = (position[None, :] < lengths_all[:, None]).astype(jnp.float32).reshape(tokens, 1)
    allowed = (position[None, None, :] <= position[None, :, None]) & (
        position[None, None, :] < lengths_all[:, None, None]
    )
    unit_rows, _ = normalize(inputs)
    normed_one = (unit_rows * gain_one + shift_one).astype(jnp.bfloat16)
    normed_two = (unit_rows * gain_two + shift_two).astype(jnp.bfloat16)
    projected = jnp.dot(normed_one, qkv_weight, preferred_element_type=jnp.float32) + qkv_bias
    projected = projected.reshape(group, length, 3, heads, HD)
    cosine_table, sine_table = rotary_tables(length)
    query_heads = rotate(projected[:, :, 0], cosine_table, sine_table).astype(jnp.bfloat16)
    key_heads = rotate(projected[:, :, 1], cosine_table, sine_table).astype(jnp.bfloat16)
    value_heads = projected[:, :, 2].astype(jnp.bfloat16)
    scores = jnp.einsum(
        "gqhd,gkhd->ghqk", query_heads, key_heads, preferred_element_type=jnp.float32
    ) * HD ** (-0.5)
    scores = jnp.where(allowed[:, None], scores, -1e30)
    row_top = jnp.max(scores, axis=-1, keepdims=True)
    raised = jnp.exp(scores - row_top)
    attend = raised / jnp.sum(raised, axis=-1, keepdims=True)
    attend_low = attend.astype(jnp.bfloat16)
    mixed = jnp.einsum(
        "ghqk,gkhd->gqhd", attend_low, value_heads, preferred_element_type=jnp.float32
    )
    mixed = mixed.reshape(tokens, head_cols).astype(jnp.bfloat16)
    hidden = jnp.dot(normed_two, up_weight, preferred_element_type=jnp.float32) + up_bias
    activated = jax.nn.gelu(hidden, approximate=False).astype(jnp.bfloat16)
    out_part = jnp.dot(mixed, out_weight, preferred_element_type=jnp.float32) + jnp.dot(
        activated, down_weight, preferred_element_type=jnp.float32
    )
    back = (cotangent_all.reshape(tokens, D).astype(jnp.float32) * live).astype(jnp.bfloat16)
    d_hidden = (against(back, down_weight) * gelu_slope(hidden)).astype(jnp.bfloat16)
    d_mixed = against(back, out_weight).astype(jnp.bfloat16).reshape(group, length, heads, HD)
    d_attend = jnp.einsum(
        "gqhd,gkhd->ghqk", d_mixed, value_heads, preferred_element_type=jnp.float32
    )
    row_inner = jnp.sum(attend * d_attend, axis=-1, keepdims=True)
    d_scores = (attend * (d_attend - row_inner)).astype(jnp.bfloat16)
    d_queries = jnp.einsum(
        "ghqk,gkhd->gqhd", d_scores, key_heads, preferred_element_type=jnp.float32
    ) * HD ** (-0.5)
    d_keys = jnp.einsum(
        "ghqk,gqhd->gkhd", d_scores, query_heads, preferred_element_type=jnp.float32
    ) * HD ** (-0.5)
    d_values = jnp.einsum(
        "ghqk,gqhd->gkhd", attend_low, d_mixed, preferred_element_type=jnp.float32
    )
    d_projected = jnp.stack(
        [
            rotate_back(d_queries, cosine_table, sine_table),
            rotate_back(d_keys, cosine_table, sine_table),
            d_values,
        ],
        axis=2,
    )
    d_projected = d_projected.reshape(tokens, 3 * head_cols).astype(jnp.bfloat16)
    d_normed_one = against(d_projected, qkv_weight)
    d_normed_two = against(d_hidden, up_weight)
    scaled_part = d_normed_one * gain_one + d_normed_two * gain_two
    norm_sums = jnp.stack(
        [
            jnp.sum(d_normed_one * unit_rows, axis=0),
            jnp.sum(d_normed_one, axis=0),
            jnp.sum(d_normed_two * unit_rows, axis=0),
            jnp.sum(d_normed_two, axis=0),
        ]
    )
    d_qkv_bias = jnp.sum(d_projected, axis=0, dtype=jnp.float32)
    d_up_bias = jnp.sum(d_hidden, axis=0, dtype=jnp.float32)
    terms = (
        outer_sum(normed_one, d_projected),
        outer_sum(mixed, back),
        outer_sum(normed_two, d_hidden),
        outer_sum(activated, back),
    )
    return (
        out_part.astype(jnp.bfloat16),
        scaled_part.astype(jnp.bfloat16),
        tuple((term.astype(jnp.bfloat16) for term in terms)),
        (norm_sums, d_qkv_bias, d_up_bias),
    )


def local_split(
    tokens_in,
    cotangent,
    lengths,
    qkv_master,
    out_master,
    up_master,
    down_master,
    small_master,
    qkv_first,
    out_first,
    up_first,
    down_first,
    small_first,
    qkv_second,
    out_second,
    up_second,
    down_second,
    small_second,
):
    masters = (qkv_master, out_master, up_master, down_master, small_master)
    firsts = (qkv_first, out_first, up_first, down_first, small_first)
    seconds = (qkv_second, out_second, up_second, down_second, small_second)
    parts, shards = (lax.axis_size("dp"), lax.axis_size("fsdp"))
    part, shard = (lax.axis_index("dp"), lax.axis_index("fsdp"))
    length = tokens_in.shape[1]
    head_cols = D // parts
    ff_cols = FF // parts
    ff_rows = down_master.shape[0] // parts
    qkv_own = sliced(qkv_master, part, parts, 3).astype(jnp.bfloat16)
    up_own = sliced(up_master, part, parts, shards).astype(jnp.bfloat16)
    down_own = lax.dynamic_slice_in_dim(down_master, part * ff_rows, ff_rows).astype(jnp.bfloat16)
    out_own = out_master.astype(jnp.bfloat16)
    small_own = small_master.astype(jnp.bfloat16)

    def over_shards(own):
        return lax.all_gather(own, "fsdp", axis=0, tiled=True)

    x_all = lax.all_gather(tokens_in, "dp", axis=0, tiled=True)
    cotangent_all = lax.all_gather(cotangent, "dp", axis=0, tiled=True)
    lengths_all = lax.all_gather(lengths, "dp", axis=0, tiled=True)
    qkv_weight, up_weight, down_weight = (over_shards(w) for w in (qkv_own, up_own, down_own))
    out_weight = lax.dynamic_slice_in_dim(over_shards(out_own), part * head_cols, head_cols)
    gain_one, shift_one, gain_two, shift_two, qkv_bias, out_bias, up_bias, down_bias = split_small(
        over_shards(small_own).astype(jnp.float32)
    )
    qkv_bias = sliced(qkv_bias[None], part, parts, 3)[0]
    up_bias = sliced(up_bias[None], part, parts, shards)[0]
    out_part, scaled_part, terms, sums = layer(
        x_all,
        cotangent_all,
        lengths_all,
        (qkv_weight, out_weight, up_weight, down_weight),
        (gain_one, shift_one, gain_two, shift_two, qkv_bias, up_bias),
        part,
    )
    out_sum = lax.psum_scatter(out_part, "dp", scatter_dimension=0, tiled=True)
    scaled = lax.psum_scatter(scaled_part, "dp", scatter_dimension=0, tiled=True)
    out_sum, scaled = (out_sum.astype(jnp.float32), scaled.astype(jnp.float32))
    inputs = tokens_in[0].astype(jnp.float32)
    live = (jnp.arange(length) < lengths[0]).astype(jnp.float32)[:, None]
    back = cotangent[0].astype(jnp.float32) * live
    unit_rows, inverse_rows = normalize(inputs)
    output = ((inputs + out_sum + out_bias + down_bias) * live).astype(jnp.bfloat16)
    input_grad = back + inverse_rows * (
        scaled
        - jnp.mean(scaled, axis=-1, keepdims=True)
        - unit_rows * jnp.mean(scaled * unit_rows, axis=-1, keepdims=True)
    )
    norm_sums, d_qkv_bias, d_up_bias = sums
    back_total = jnp.sum(back, axis=0)

    def spread(values, pieces):
        wide = jnp.zeros((pieces, parts, values.shape[0] // pieces), jnp.float32)
        return lax.dynamic_update_index_in_dim(
            wide, values.reshape(pieces, -1), part, axis=1
        ).reshape(-1)

    small_grad = jnp.concatenate(
        [
            norm_sums.reshape(4 * D),
            spread(d_qkv_bias, 3),
            back_total,
            spread(d_up_bias, shards),
            back_total,
        ]
    )
    small_sum = lax.psum(small_grad, ("dp", "fsdp"))
    small_rows = small_master.shape[0]
    small_sum = lax.dynamic_slice_in_dim(small_sum, shard * small_rows, small_rows)
    qkv_term, out_term, up_term, down_term = terms
    out_wide = lax.dynamic_update_slice_in_dim(
        jnp.zeros((D, D), jnp.bfloat16), out_term, part * head_cols, axis=0
    )

    def to_owner(term):
        own = lax.psum_scatter(term, "fsdp", scatter_dimension=0, tiled=True)
        return lax.all_gather(own, "dp", axis=0, tiled=False).astype(jnp.float32)

    qkv_sum = joined(to_owner(qkv_term), 3)
    up_sum = joined(to_owner(up_term), shards)
    down_sum = to_owner(down_term).reshape(down_master.shape)
    out_sum_grad = lax.psum(
        lax.psum_scatter(out_wide, "fsdp", scatter_dimension=0, tiled=True), "dp"
    ).astype(jnp.float32)
    reduced = (qkv_sum, out_sum_grad, up_sum, down_sum, small_sum)
    return (output[None], input_grad.astype(jnp.bfloat16)[None]) + lamb(
        masters, firsts, seconds, reduced
    )


def lamb(masters, firsts, seconds, reduced):
    updates = []
    first_news = []
    second_news = []
    for first_old, second_old, master, grad_sum in zip(firsts, seconds, masters, reduced):
        first_new = BETA_ONE * first_old + (1.0 - BETA_ONE) * grad_sum
        second_new = BETA_TWO * second_old + (1.0 - BETA_TWO) * grad_sum * grad_sum
        updates.append(first_new / (jnp.sqrt(second_new) + ADAM_EPSILON) + DECAY * master)
        first_news.append(first_new)
        second_news.append(second_new)
    weight_squares, update_squares = lax.psum(
        (local_squares(masters), local_squares(updates)), "fsdp"
    )
    weight_norms = jnp.sqrt(weight_squares)
    update_norms = jnp.sqrt(update_squares)
    new_masters = [
        masters[number] - RATE * (weight_norms[number] / update_norms[number]) * updates[number]
        for number in range(5)
    ]
    lamb_norms = jnp.stack([weight_norms, update_norms])
    return tuple(new_masters) + tuple(first_news) + tuple(second_news) + (lamb_norms,)


def solution(mesh):
    in_specs = (
        P(("dp", "fsdp"), None, None),
        P(("dp", "fsdp"), None, None),
        P(("dp", "fsdp")),
        P("fsdp", None),
        P("fsdp", None),
        P("fsdp", None),
        P("fsdp", None),
        P("fsdp"),
        P("fsdp", None),
        P("fsdp", None),
        P("fsdp", None),
        P("fsdp", None),
        P("fsdp"),
        P("fsdp", None),
        P("fsdp", None),
        P("fsdp", None),
        P("fsdp", None),
        P("fsdp"),
    )
    out_specs = (
        P(("dp", "fsdp"), None, None),
        P(("dp", "fsdp"), None, None),
        P("fsdp", None),
        P("fsdp", None),
        P("fsdp", None),
        P("fsdp", None),
        P("fsdp"),
        P("fsdp", None),
        P("fsdp", None),
        P("fsdp", None),
        P("fsdp", None),
        P("fsdp"),
        P("fsdp", None),
        P("fsdp", None),
        P("fsdp", None),
        P("fsdp", None),
        P("fsdp"),
        P(),
    )
    return jax.shard_map(
        local_split, mesh=mesh, in_specs=in_specs, out_specs=out_specs, check_vma=False
    )
```

profile of v0, /device:TPU:0, one launch (start us, length us, event | category | flops | bytes accessed | tf_op | source)
XLA Modules:
  0.0 634.2 jit_solution(11582230660681982558)
XLA Ops:
  17.1 15.7 %all-gather.3 = bf16[8,1,1664]{2,1,0:T(2,128)(2,1)S(1)} all-gather(bf16[1,1,1664]{2,1,0:T(2,128)(2,1)S(1)} %reshape.376), channel_id=1, replica_groups=mesh['dp'=4,'fsdp'=8] {'fsdp'}, dimensions={0}, use_global_device_ids=true | all-gather | bytes 29952 | tf_op jit(solution)/shard_map/all_gather | solution.py:238
  36.3 8.1 %all-reduce = s32[4]{0:T(128)S(1)} all-reduce(s32[4]{0:T(128)S(1)} %dynamic-update-slice), channel_id=1, replica_groups=mesh['dp'=4,'fsdp'=8] {'dp'}, use_global_device_ids=true, to_apply=%add | all-reduce | flops 4 | bytes 32
  54.4 23.0 %all-gather.15.cloned.1.call-done = bf16[1024,768]{0,1:T(8,128)(2,1)} async-done(((bf16[128,768]{0,1:T(8,128)(2,1)}), bf16[1024,768]{0,1:T(8,128)(2,1)}) %all-gather.15.cloned.1.call-update) | async-done | bytes 1572880 | tf_op jit(solution)/shard_map/all_gather | solution.py:238
  77.4 5.6 convolution_add_fusion
  82.9 6.4 %reshape.381 = f32[4,256,3,4,64]{4,3,2,1,0:T(4,128)} reshape(f32[1024,768]{1,0:T(8,128)} %convolution_add_fusion) | data formatting | bytes 6291456 | tf_op jit(solution)/shard_map/reshape | solution.py:127
  91.3 4.5 fusion.75
  106.7 5.2 fusion.79
  124.9 21.7 %all-gather.19.cloned.1.call-done = bf16[1024,1024]{0,1:T(8,128)(2,1)} async-done(((bf16[128,1024]{0,1:T(8,128)(2,1)}), bf16[1024,1024]{0,1:T(8,128)(2,1)}) %all-gather.19.cloned.1.call-update) | async-done | bytes 2097168 | tf_op jit(solution)/shard_map/all_gather | solution.py:238
  146.6 14.6 %fusion.3 = (bf16[1024,1024]{1,0:T(8,128)(2,1)}, f32[1024,1024]{1,0:T(8,128)}) fusion(f32[1024]{0:T(1024)S(1)} %bitcast.220, bf16[1024,1024]{1,0:T(8,128)(2,1)} %get-tuple-element.89, bf16[1024,1024]{0,1:T(8,128)(2,1)} %all-gather.19.cloned.1.call-done), kind=kOutput, calls=%fused_computation.5 | convolution fusion | flops 2216689664 | bytes 10489856 | tf_op jit(solution)/shard_map/dot_general | solution.py:144
  161.2 15.7 %all-gather.21.cloned.1.call-done = bf16[1024,1024]{1,0:T(8,128)(2,1)} async-done(((bf16[128,1024]{1,0:T(8,128)(2,1)}), bf16[1024,1024]{1,0:T(8,128)(2,1)}) %all-gather.21.cloned.1.call-update) | async-done | bytes 2097168 | tf_op jit(solution)/shard_map/all_gather | solution.py:238
  176.8 8.0 %convert_reduce_fusion = (f32[1024]{0:T(1024)}, bf16[1024,1024]{1,0:T(8,128)(2,1)}) fusion(f32[1024,1024]{1,0:T(8,128)} %get-tuple-element.138, f32[1024]{0:T(1024)S(1)} %bitcast.221, bf16[1024,1024]{1,0:T(8,128)(2,1)} %fusion.10, bf16[1024,1024]{1,0:T(8,128)(2,1)} %all-gather.21.cloned.1.call-done), kind=kOutput, calls=%fused_computation.16 | convolution fusion | flops 2161114112 | bytes 10493952 | tf_op jit(solution)/shard_map/dot_general | solution.py:77
  184.9 30.0 %reduce-scatter.13.cloned.1.call-done = bf16[128,1024]{1,0:T(8,128)(2,1)} async-done(((bf16[1024,1024]{1,0:T(8,128)(2,1)}), bf16[128,1024]{1,0:T(8,128)(2,1)}) %reduce-scatter.13.cloned.1.call-update) | async-done | bytes 262160 | tf_op jit(solution)/shard_map/reduce_scatter | solution.py:305
  214.9 5.9 convolution_convert_fusion.1
  221.2 6.0 convolution_convert_fusion
  227.2 32.3 %all-reduce.4.cloned.1.call-done = bf16[128,1024]{1,0:T(8,128)(2,1)} async-done(((bf16[128,1024]{1,0:T(8,128)(2,1)}), bf16[128,1024]{1,0:T(8,128)(2,1)}) %all-reduce.4.cloned.1.call-update) | async-done | bytes 262160 | tf_op jit(solution)/shard_map/psum | solution.py:304
  262.6 35.6 %reduce-scatter.15.cloned.1.call-done = bf16[128,1024]{1,0:T(8,128)(2,1)} async-done(((bf16[1024,1024]{1,0:T(8,128)(2,1)}), bf16[128,1024]{1,0:T(8,128)(2,1)}) %reduce-scatter.15.cloned.1.call-update) | async-done | bytes 262160 | tf_op jit(solution)/shard_map/reduce_scatter | solution.py:298
  301.2 34.5 %reduce-scatter.17.cloned.1.call-done = bf16[128,1024]{1,0:T(8,128)(2,1)} async-done(((bf16[1024,1024]{1,0:T(8,128)(2,1)}), bf16[128,1024]{1,0:T(8,128)(2,1)}) %reduce-scatter.17.cloned.1.call-update) | async-done | bytes 262160 | tf_op jit(solution)/shard_map/reduce_scatter | solution.py:298
  335.8 29.7 %all-gather.17.cloned.1.call-done = bf16[1024,1024]{1,0:T(8,128)(2,1)} async-done(((bf16[128,1024]{1,0:T(8,128)(2,1)}), bf16[1024,1024]{1,0:T(8,128)(2,1)}) %all-gather.17.cloned.1.call-update) | async-done | bytes 2097168 | tf_op jit(solution)/shard_map/all_gather | solution.py:238
  387.5 4.7 fusion.81
  392.3 4.3 multiply_reduce_fusion.1
  403.1 4.6 fusion.80
  422.2 7.5 %multiply_reduce_fusion.4 = (f32[]{:T(128)}, f32[]{:T(128)}, f32[512,1024]{1,0:T(8,128)}, f32[512,1024]{1,0:T(8,128)}) fusion(f32[512,1024]{1,0:T(8,128)} %param.24, bf16[512,1024]{1,0:T(8,128)(2,1)} %all-gather.27.cloned.1.call-done, f32[512,1024]{1,0:T(8,128)} %param.34, f32[512,1024]{1,0:T(8,128)} %param.29), kind=kLoop, calls=%fused_computation.61 | loop fusion | flops 7864318 | bytes 11534344 | tf_op jit(solution)/shard_map/reduce_sum | solution.py:89
  429.8 4.1 multiply_reduce_fusion.5
  434.1 25.4 %reduce-scatter.11.cloned.1.call-done = bf16[128,768]{1,0:T(8,128)(2,1)} async-done(((bf16[1024,768]{1,0:T(8,128)(2,1)}), bf16[128,768]{1,0:T(8,128)(2,1)}) %reduce-scatter.11.cloned.1.call-update) | async-done | bytes 196624 | tf_op jit(solution)/shard_map/reduce_scatter | solution.py:298
  459.4 14.9 %all-gather = bf16[512,768]{1,0:T(8,128)(2,1)S(1)} all-gather(bf16[128,768]{1,0:T(8,128)(2,1)} %reduce-scatter.11.cloned.1.call-done), channel_id=2, replica_groups=mesh['dp'=4,'fsdp'=8] {'dp'}, dimensions={0}, use_global_device_ids=true | all-gather | bytes 983040 | tf_op jit(solution)/shard_map/all_gather | solution.py:299
  480.9 4.9 multiply_reduce_fusion.8
  488.9 7.5 %reduce-scatter.9.cloned.1.call-done = bf16[256,1024]{1,0:T(8,128)(2,1)} async-done(((bf16[1024,1024]{1,0:T(8,128)(2,1)}), bf16[256,1024]{1,0:T(8,128)(2,1)}) %reduce-scatter.9.cloned.1.call-update) | async-done | bytes 524304 | tf_op jit(solution)/shard_map/reduce_scatter | solution.py:259
  497.8 37.1 %reduce-scatter.7.cloned.1.call-done = bf16[256,1024]{1,0:T(8,128)(2,1)} async-done(((bf16[1024,1024]{1,0:T(8,128)(2,1)}), bf16[256,1024]{1,0:T(8,128)(2,1)}) %reduce-scatter.7.cloned.1.call-update) | async-done | bytes 524304 | tf_op jit(solution)/shard_map/reduce_scatter | solution.py:258
  537.7 39.9 %psum.30 = f32[13312]{0:T(1024)S(1)} all-reduce(f32[13312]{0:T(1024)S(1)} %constant_dynamic-update-slice_fusion), channel_id=1, replica_groups=mesh['dp'=4,'fsdp'=8] {'dp','fsdp'}, use_global_device_ids=true, to_apply=%region_33.34 | all-reduce | flops 13312 | bytes 106496 | tf_op jit(solution)/shard_map/psum | solution.py:289
  588.0 14.7 %all-reduce.1 = (f32[5]{0:T(128)S(1)}, f32[5]{0:T(128)S(1)}) all-reduce(f32[5]{0:T(128)S(1)} %stack.81, f32[5]{0:T(128)S(1)} %stack.92), channel_id=1, replica_groups=mesh['dp'=4,'fsdp'=8] {'fsdp'}, use_global_device_ids=true, to_apply=%region_16.17 | all-reduce | flops 10 | bytes 80 | tf_op jit(solution)/shard_map/psum | solution.py:323
  610.3 4.2 multiply_subtract_fusion.2
  618.7 5.4 multiply_subtract_fusion
  (262 shorter events, 130.7 us)
Async XLA Ops:
  7.2 40.8 %all-gather.13.cloned.1.call-start = ((), (), s32[]{:S(2)}) async-start(), calls=%async_computation.6 | async-start | bytes 2621440 | tf_op jit(solution)/shard_map/all_gather | solution.py:240
  7.9 69.4 %all-gather.15.cloned.1.call-start = ((), (), s32[]{:S(2)}) async-start(), calls=%async_computation.7 | async-start | bytes 1769472 | tf_op jit(solution)/shard_map/all_gather | solution.py:238
  12.9 102.3 %all-gather.23.cloned.1.call-start = ((), (), s32[]{:S(2)}) async-start(), calls=%async_computation.12 | async-start | bytes 2621440 | tf_op jit(solution)/shard_map/all_gather | solution.py:241
  13.6 21.3 %copy-start.58 = (u32[32]{0:T(128)S(1)}, u32[32]{0:T(128)}, u32[]{:S(2)}) copy-start(u32[32]{0:T(128)} %constant.166) | copy-start | bytes 388
  13.6 133.0 %all-gather.19.cloned.1.call-start = ((), (), s32[]{:S(2)}) async-start(), calls=%async_computation.9 | async-start | bytes 2359296 | tf_op jit(solution)/shard_map/all_gather | solution.py:238
  15.2 161.6 %all-gather.21.cloned.1.call-start = ((), (), s32[]{:S(2)}) async-start(), calls=%async_computation.10 | async-start | bytes 2359296 | tf_op jit(solution)/shard_map/all_gather | solution.py:238
  17.1 197.8 %reduce-scatter.13.cloned.1.call-start = ((), (), s32[]{:S(2)}) async-start(), calls=%async_computation.15 | async-start | bytes 2359296 | tf_op jit(solution)/shard_map/reduce_scatter | solution.py:305
  33.5 18.1 %copy-start.38 = (f32[1024]{0:T(1024)}, f32[1024]{0:T(1024)S(1)}, u32[]{:S(2)}) copy-start(f32[1024]{0:T(1024)S(1)} %get-tuple-element.107) | copy-start | bytes 12292
  33.5 18.1 %copy-start.40 = (f32[1024]{0:T(1024)}, f32[1024]{0:T(1024)S(1)}, u32[]{:S(2)}) copy-start(f32[1024]{0:T(1024)S(1)} %get-tuple-element.106) | copy-start | bytes 12292
  33.5 18.1 %copy-start.47 = (f32[1024]{0:T(1024)}, f32[1024]{0:T(1024)S(1)}, u32[]{:S(2)}) copy-start(f32[1024]{0:T(1024)S(1)} %get-tuple-element.105) | copy-start | bytes 12292
  120.6 138.9 %all-reduce.4.cloned.1.call-start = ((), (), s32[]{:S(2)}) async-start(), calls=%async_computation.16 | async-start | bytes 524288 | tf_op jit(solution)/shard_map/psum | solution.py:304
  214.9 83.4 %reduce-scatter.15.cloned.1.call-start = ((), (), s32[]{:S(2)}) async-start(), calls=%async_computation.17 | async-start | bytes 2359296 | tf_op jit(solution)/shard_map/reduce_scatter | solution.py:298
  220.9 114.8 %reduce-scatter.17.cloned.1.call-start = ((), (), s32[]{:S(2)}) async-start(), calls=%async_computation.18 | async-start | bytes 2359296 | tf_op jit(solution)/shard_map/reduce_scatter | solution.py:298
  227.1 32.3 %copy-start.14 = (f32[128,1024]{1,0:T(8,128)S(1)}, f32[128,1024]{1,0:T(8,128)}, u32[]{:S(2)}) copy-start(f32[128,1024]{1,0:T(8,128)} %param.22) | copy-start | bytes 1572868
  227.1 32.3 %copy-start.27 = (f32[128,1024]{1,0:T(8,128)S(1)}, f32[128,1024]{1,0:T(8,128)}, u32[]{:S(2)}) copy-start(f32[128,1024]{1,0:T(8,128)} %param.32) | copy-start | bytes 1572868
  227.2 138.3 %all-gather.17.cloned.1.call-start = ((), (), s32[]{:S(2)}) async-start(), calls=%async_computation.8 | async-start | bytes 2359296 | tf_op jit(solution)/shard_map/all_gather | solution.py:238
  262.6 150.9 %all-gather.25.cloned.1.call-start = ((), (), s32[]{:S(2)}) async-start(), calls=%async_computation.19 | async-start | bytes 1310720 | tf_op jit(solution)/shard_map/all_gather | solution.py:299
  298.3 123.9 %all-gather.27.cloned.1.call-start = ((), (), s32[]{:S(2)}) async-start(), calls=%async_computation.20 | async-start | bytes 1310720 | tf_op jit(solution)/shard_map/all_gather | solution.py:299
  335.8 123.7 %reduce-scatter.11.cloned.1.call-start = ((), (), s32[]{:S(2)}) async-start(), calls=%async_computation.14 | async-start | bytes 1769472 | tf_op jit(solution)/shard_map/reduce_scatter | solution.py:298
  387.0 109.3 %reduce-scatter.9.cloned.1.call-start = ((), (), s32[]{:S(2)}) async-start(), calls=%async_computation.13 | async-start | bytes 2621440 | tf_op jit(solution)/shard_map/reduce_scatter | solution.py:259
  396.5 138.4 %reduce-scatter.7.cloned.1.call-start = ((), (), s32[]{:S(2)}) async-start(), calls=%async_computation.11 | async-start | bytes 2621440 | tf_op jit(solution)/shard_map/reduce_scatter | solution.py:258
  419.0 10.8 %copy-start.2 = (f32[128,4096]{1,0:T(8,128)S(1)}, f32[128,4096]{1,0:T(8,128)}, u32[]{:S(2)}) copy-start(f32[128,4096]{1,0:T(8,128)} %param.23) | copy-start | bytes 6291460
  422.2 7.5 %copy-start.11 = (f32[128,4096]{1,0:T(8,128)S(1)}, f32[128,4096]{1,0:T(8,128)}, u32[]{:S(2)}) copy-start(f32[128,4096]{1,0:T(8,128)} %param.33) | copy-start | bytes 6291460
  422.2 7.5 %copy-start.12 = (f32[128,4096]{1,0:T(8,128)S(1)}, f32[128,4096]{1,0:T(8,128)}, u32[]{:S(2)}) copy-start(f32[128,4096]{1,0:T(8,128)} %param.28) | copy-start | bytes 6291460
  485.8 49.2 %copy-start.18 = (bf16[1,256,1024]{2,1,0:T(8,128)(2,1)S(1)}, bf16[1,256,1024]{2,1,0:T(8,128)(2,1)}, u32[]{:S(2)}) copy-start(bf16[1,256,1024]{2,1,0:T(8,128)(2,1)} %param.19) | copy-start | bytes 1572868
  485.8 49.2 %copy-start.45 = (f32[1024]{0:T(1024)S(1)}, f32[1024]{0:T(1024)}, u32[]{:S(2)}) copy-start(f32[1024]{0:T(1024)} %get-tuple-element.102) | copy-start | bytes 12292
  485.8 49.2 %copy-start.46 = (f32[1024]{0:T(1024)S(1)}, f32[1024]{0:T(1024)}, u32[]{:S(2)}) copy-start(f32[1024]{0:T(1024)} %get-tuple-element.103) | copy-start | bytes 12292
  488.9 88.7 %copy-start.37 = (f32[1664]{0:T(1024)S(1)}, f32[1664]{0:T(1024)}, u32[]{:S(2)}) copy-start(f32[1664]{0:T(1024)} %param.25) | copy-start | bytes 19972
  488.9 88.7 %copy-start.54 = (f32[1664]{0:T(1024)S(1)}, f32[1664]{0:T(1024)}, u32[]{:S(2)}) copy-start(f32[1664]{0:T(1024)} %param.35) | copy-start | bytes 19972
  488.9 88.7 %copy-start.55 = (f32[1664]{0:T(1024)S(1)}, f32[1664]{0:T(1024)}, u32[]{:S(2)}) copy-start(f32[1664]{0:T(1024)} %param.30) | copy-start | bytes 19972
  578.3 39.8 %copy-start.42 = (f32[1664]{0:T(1024)}, f32[1664]{0:T(1024)S(1)}, u32[]{:S(2)}) copy-start(f32[1664]{0:T(1024)S(1)} %get-tuple-element.75) | copy-start | bytes 19972
  578.3 39.8 %copy-start.43 = (f32[1664]{0:T(1024)}, f32[1664]{0:T(1024)S(1)}, u32[]{:S(2)}) copy-start(f32[1664]{0:T(1024)S(1)} %get-tuple-element.76) | copy-start | bytes 19972
  (42 other events, 144.1 us)
Sparse Core Ops, SparseCore 0:
  9.9 38.0 all-gather.12
  50.2 27.1 all-gather.14
  79.2 34.4 all-gather.22
  115.7 30.8 all-gather.18
  148.6 28.1 all-gather.20
  179.5 35.2 reduce-scatter.12
  217.8 41.6 all-reduce.3
  262.4 35.7 reduce-scatter.14
  301.2 34.4 reduce-scatter.16
  337.8 27.6 all-gather.16
  367.5 26.1 all-gather.24
  395.5 26.6 all-gather.26
  425.2 34.1 reduce-scatter.10
  463.1 33.1 reduce-scatter.8
  499.7 35.1 reduce-scatter.6
where the time goes:
time: 638 us; the launch traced here: 634 us
  waiting for transfers between devices  299 us (47%)
  blocking collectives  93.2 us (15%)
  local copies, waits for them, and re-layouts  80.2 us (13%)
  matrix products  78.1 us (12%)
  other arithmetic  60.6 us (9%)
  between operations  22 us (3%)
    reduce_scatter x3, waiting for transfers between devices, to_owner(): own = lax.psum_scatter(term, 'fsdp', scatter_dimension=0, tiled=True)  95.5 us
    all_gather x4, waiting for transfers between devices, over_shards(): return lax.all_gather(own, 'fsdp', axis=0, tiled=True)  90 us
    psum x1, blocking collectives, local_split(): small_sum = lax.psum(small_grad, ('dp', 'fsdp'))  39.9 us
    reduce_scatter x1, waiting for transfers between devices, local_split(): out_sum = lax.psum_scatter(out_part, 'dp', scatter_dimension=0, tiled=True)  37.1 us
    unnamed x143, local copies, waits for them, and re-layouts  33.9 us
    psum x1, waiting for transfers between devices, local_split(): lax.psum(lax.psum_scatter(out_wide, 'fsdp', scatter_dimension=0, tiled=Tr...  32.3 us
    reduce_scatter x1, waiting for transfers between devices, local_split(): lax.psum_scatter(out_wide, 'fsdp', scatter_dimension=0, tiled=True)  30 us
    reduce_sum x6, other arithmetic, local_squares(): return jnp.stack([jnp.sum(array_in * array_in) for array_in in arrays])  21.3 us
  transfers between devices with their start and end apart: 15, of which 13 were waited for; matrix products, arithmetic and copies ran while one was open for 28% of the time, Pallas kernels for 0%

commit v1 on v0

--- a/solution.py
+++ b/solution.py
@@ -286,7 +286,7 @@
             back_total,
         ]
     )
-    small_sum = lax.psum(small_grad, ("dp", "fsdp"))
+    small_sum = lax.psum(lax.psum(small_grad, "fsdp"), "dp")
     small_rows = small_master.shape[0]
     small_sum = lax.dynamic_slice_in_dim(small_sum, shard * small_rows, small_rows)
     qkv_term, out_term, up_term, down_term = terms

time: 638 us -> 643 us (level)
    psum x1 -> x2, blocking collectives: 39.9 us -> 45.1 us  [local_split(): small_sum = lax.psum(lax.psum(small_grad, 'fsdp'), 'dp')]
where the time goes in v1:
time: 643 us; the launch traced here: 639 us
  waiting for transfers between devices  299 us (47%)
  blocking collectives  97.5 us (15%)
  local copies, waits for them, and re-layouts  80.1 us (12%)
  matrix products  78.2 us (12%)
  other arithmetic  60.6 us (9%)
  between operations  22.2 us (3%)
    reduce_scatter x3, waiting for transfers between devices, to_owner(): own = lax.psum_scatter(term, 'fsdp', scatter_dimension=0, tiled=True)  95.6 us
    all_gather x4, waiting for transfers between devices, over_shards(): return lax.all_gather(own, 'fsdp', axis=0, tiled=True)  90 us
    psum x2, blocking collectives, local_split(): small_sum = lax.psum(lax.psum(small_grad, 'fsdp'), 'dp')  45.1 us
    reduce_scatter x1, waiting for transfers between devices, local_split(): out_sum = lax.psum_scatter(out_part, 'dp', scatter_dimension=0, tiled=True)  37.1 us
    unnamed x143, local copies, waits for them, and re-layouts  33.9 us
    psum x1, waiting for transfers between devices, local_split(): lax.psum(lax.psum_scatter(out_wide, 'fsdp', scatter_dimension=0, tiled=Tr...  32.3 us
    reduce_scatter x1, waiting for transfers between devices, local_split(): lax.psum_scatter(out_wide, 'fsdp', scatter_dimension=0, tiled=True)  30 us
    reduce_sum x6, other arithmetic, local_squares(): return jnp.stack([jnp.sum(array_in * array_in) for array_in in arrays])  21.3 us
  transfers between devices with their start and end apart: 15, of which 13 were waited for; matrix products, arithmetic and copies ran while one was open for 28% of the time, Pallas kernels for 0%

profile of v1, /device:TPU:0, one launch (start us, length us, event | category | flops | bytes accessed | tf_op | source)
XLA Modules:
  0.0 638.7 jit_solution(6188957719658167694)
XLA Ops:
  17.1 15.7 %all-gather.3 = bf16[8,1,1664]{2,1,0:T(2,128)(2,1)S(1)} all-gather(bf16[1,1,1664]{2,1,0:T(2,128)(2,1)S(1)} %reshape.376), channel_id=1, replica_groups=mesh['dp'=4,'fsdp'=8] {'fsdp'}, dimensions={0}, use_global_device_ids=true | all-gather | bytes 29952 | tf_op jit(solution)/shard_map/all_gather | solution.py:238
  36.3 8.1 %all-reduce = s32[4]{0:T(128)S(1)} all-reduce(s32[4]{0:T(128)S(1)} %dynamic-update-slice), channel_id=1, replica_groups=mesh['dp'=4,'fsdp'=8] {'dp'}, use_global_device_ids=true, to_apply=%add | all-reduce | flops 4 | bytes 32
  54.4 23.0 %all-gather.15.cloned.1.call-done = bf16[1024,768]{0,1:T(8,128)(2,1)} async-done(((bf16[128,768]{0,1:T(8,128)(2,1)}), bf16[1024,768]{0,1:T(8,128)(2,1)}) %all-gather.15.cloned.1.call-update) | async-done | bytes 1572880 | tf_op jit(solution)/shard_map/all_gather | solution.py:238
  77.4 5.6 convolution_add_fusion
  82.9 6.4 %reshape.381 = f32[4,256,3,4,64]{4,3,2,1,0:T(4,128)} reshape(f32[1024,768]{1,0:T(8,128)} %convolution_add_fusion) | data formatting | bytes 6291456 | tf_op jit(solution)/shard_map/reshape | solution.py:127
  91.3 4.5 fusion.75
  106.7 5.3 fusion.79
  124.9 21.7 %all-gather.19.cloned.1.call-done = bf16[1024,1024]{0,1:T(8,128)(2,1)} async-done(((bf16[128,1024]{0,1:T(8,128)(2,1)}), bf16[1024,1024]{0,1:T(8,128)(2,1)}) %all-gather.19.cloned.1.call-update) | async-done | bytes 2097168 | tf_op jit(solution)/shard_map/all_gather | solution.py:238
  146.6 14.6 %fusion.3 = (bf16[1024,1024]{1,0:T(8,128)(2,1)}, f32[1024,1024]{1,0:T(8,128)}) fusion(f32[1024]{0:T(1024)S(1)} %bitcast.220, bf16[1024,1024]{1,0:T(8,128)(2,1)} %get-tuple-element.89, bf16[1024,1024]{0,1:T(8,128)(2,1)} %all-gather.19.cloned.1.call-done), kind=kOutput, calls=%fused_computation.5 | convolution fusion | flops 2216689664 | bytes 10489856 | tf_op jit(solution)/shard_map/dot_general | solution.py:144
  161.2 15.7 %all-gather.21.cloned.1.call-done = bf16[1024,1024]{1,0:T(8,128)(2,1)} async-done(((bf16[128,1024]{1,0:T(8,128)(2,1)}), bf16[1024,1024]{1,0:T(8,128)(2,1)}) %all-gather.21.cloned.1.call-update) | async-done | bytes 2097168 | tf_op jit(solution)/shard_map/all_gather | solution.py:238
  176.8 8.0 %convert_reduce_fusion = (f32[1024]{0:T(1024)}, bf16[1024,1024]{1,0:T(8,128)(2,1)}) fusion(f32[1024,1024]{1,0:T(8,128)} %get-tuple-element.138, f32[1024]{0:T(1024)S(1)} %bitcast.221, bf16[1024,1024]{1,0:T(8,128)(2,1)} %fusion.10, bf16[1024,1024]{1,0:T(8,128)(2,1)} %all-gather.21.cloned.1.call-done), kind=kOutput, calls=%fused_computation.16 | convolution fusion | flops 2161114112 | bytes 10493952 | tf_op jit(solution)/shard_map/dot_general | solution.py:77
  184.9 30.0 %reduce-scatter.13.cloned.1.call-done = bf16[128,1024]{1,0:T(8,128)(2,1)} async-done(((bf16[1024,1024]{1,0:T(8,128)(2,1)}), bf16[128,1024]{1,0:T(8,128)(2,1)}) %reduce-scatter.13.cloned.1.call-update) | async-done | bytes 262160 | tf_op jit(solution)/shard_map/reduce_scatter | solution.py:305
  214.9 5.9 convolution_convert_fusion.1
  221.2 6.0 convolution_convert_fusion
  227.2 32.3 %all-reduce.4.cloned.1.call-done = bf16[128,1024]{1,0:T(8,128)(2,1)} async-done(((bf16[128,1024]{1,0:T(8,128)(2,1)}), bf16[128,1024]{1,0:T(8,128)(2,1)}) %all-reduce.4.cloned.1.call-update) | async-done | bytes 262160 | tf_op jit(solution)/shard_map/psum | solution.py:304
  262.7 35.6 %reduce-scatter.15.cloned.1.call-done = bf16[128,1024]{1,0:T(8,128)(2,1)} async-done(((bf16[1024,1024]{1,0:T(8,128)(2,1)}), bf16[128,1024]{1,0:T(8,128)(2,1)}) %reduce-scatter.15.cloned.1.call-update) | async-done | bytes 262160 | tf_op jit(solution)/shard_map/reduce_scatter | solution.py:298
  301.2 34.5 %reduce-scatter.17.cloned.1.call-done = bf16[128,1024]{1,0:T(8,128)(2,1)} async-done(((bf16[1024,1024]{1,0:T(8,128)(2,1)}), bf16[128,1024]{1,0:T(8,128)(2,1)}) %reduce-scatter.17.cloned.1.call-update) | async-done | bytes 262160 | tf_op jit(solution)/shard_map/reduce_scatter | solution.py:298
  335.8 29.7 %all-gather.17.cloned.1.call-done = bf16[1024,1024]{1,0:T(8,128)(2,1)} async-done(((bf16[128,1024]{1,0:T(8,128)(2,1)}), bf16[1024,1024]{1,0:T(8,128)(2,1)}) %all-gather.17.cloned.1.call-update) | async-done | bytes 2097168 | tf_op jit(solution)/shard_map/all_gather | solution.py:238
  387.5 4.7 fusion.81
  392.3 4.3 multiply_reduce_fusion.1
  403.1 4.6 fusion.80
  422.3 7.5 %multiply_reduce_fusion.4 = (f32[]{:T(128)}, f32[]{:T(128)}, f32[512,1024]{1,0:T(8,128)}, f32[512,1024]{1,0:T(8,128)}) fusion(f32[512,1024]{1,0:T(8,128)} %param.24, bf16[512,1024]{1,0:T(8,128)(2,1)} %all-gather.27.cloned.1.call-done, f32[512,1024]{1,0:T(8,128)} %param.34, f32[512,1024]{1,0:T(8,128)} %param.29), kind=kLoop, calls=%fused_computation.61 | loop fusion | flops 7864318 | bytes 11534344 | tf_op jit(solution)/shard_map/reduce_sum | solution.py:89
  434.1 25.4 %reduce-scatter.11.cloned.1.call-done = bf16[128,768]{1,0:T(8,128)(2,1)} async-done(((bf16[1024,768]{1,0:T(8,128)(2,1)}), bf16[128,768]{1,0:T(8,128)(2,1)}) %reduce-scatter.11.cloned.1.call-update) | async-done | bytes 196624 | tf_op jit(solution)/shard_map/reduce_scatter | solution.py:298
  459.5 14.9 %all-gather = bf16[512,768]{1,0:T(8,128)(2,1)S(1)} all-gather(bf16[128,768]{1,0:T(8,128)(2,1)} %reduce-scatter.11.cloned.1.call-done), channel_id=2, replica_groups=mesh['dp'=4,'fsdp'=8] {'dp'}, dimensions={0}, use_global_device_ids=true | all-gather | bytes 983040 | tf_op jit(solution)/shard_map/all_gather | solution.py:299
  481.0 4.9 multiply_reduce_fusion.8
  488.9 7.5 %reduce-scatter.9.cloned.1.call-done = bf16[256,1024]{1,0:T(8,128)(2,1)} async-done(((bf16[1024,1024]{1,0:T(8,128)(2,1)}), bf16[256,1024]{1,0:T(8,128)(2,1)}) %reduce-scatter.9.cloned.1.call-update) | async-done | bytes 524304 | tf_op jit(solution)/shard_map/reduce_scatter | solution.py:259
  497.8 37.1 %reduce-scatter.7.cloned.1.call-done = bf16[256,1024]{1,0:T(8,128)(2,1)} async-done(((bf16[1024,1024]{1,0:T(8,128)(2,1)}), bf16[256,1024]{1,0:T(8,128)(2,1)}) %reduce-scatter.7.cloned.1.call-update) | async-done | bytes 524304 | tf_op jit(solution)/shard_map/reduce_scatter | solution.py:258
  537.7 29.0 %psum.37 = f32[13312]{0:T(1024)S(1)} all-reduce(f32[13312]{0:T(1024)S(1)} %constant_dynamic-update-slice_fusion), channel_id=1, replica_groups=mesh['dp'=4,'fsdp'=8] {'fsdp'}, use_global_device_ids=true, to_apply=%region_33.34 | all-reduce | flops 13312 | bytes 106496 | tf_op jit(solution)/shard_map/psum | solution.py:289
  566.7 16.1 %psum.38 = f32[13312]{0:T(1024)S(1)} all-reduce(f32[13312]{0:T(1024)S(1)} %psum.37), channel_id=1, replica_groups=mesh['dp'=4,'fsdp'=8] {'dp'}, use_global_device_ids=true, to_apply=%region_34.35 | all-reduce | flops 13312 | bytes 106496 | tf_op jit(solution)/shard_map/psum | solution.py:289
  593.1 13.8 %all-reduce.1 = (f32[5]{0:T(128)S(1)}, f32[5]{0:T(128)S(1)}) all-reduce(f32[5]{0:T(128)S(1)} %stack.81, f32[5]{0:T(128)S(1)} %stack.92), channel_id=1, replica_groups=mesh['dp'=4,'fsdp'=8] {'fsdp'}, use_global_device_ids=true, to_apply=%region_16.17 | all-reduce | flops 10 | bytes 80 | tf_op jit(solution)/shard_map/psum | solution.py:323
  614.8 4.2 multiply_subtract_fusion.2
  623.2 5.4 multiply_subtract_fusion
  (263 shorter events, 134.7 us)
Async XLA Ops:
  7.2 40.8 %all-gather.13.cloned.1.call-start = ((), (), s32[]{:S(2)}) async-start(), calls=%async_computation.6 | async-start | bytes 2621440 | tf_op jit(solution)/shard_map/all_gather | solution.py:240
  7.9 69.4 %all-gather.15.cloned.1.call-start = ((), (), s32[]{:S(2)}) async-start(), calls=%async_computation.7 | async-start | bytes 1769472 | tf_op jit(solution)/shard_map/all_gather | solution.py:238
  12.9 102.3 %all-gather.23.cloned.1.call-start = ((), (), s32[]{:S(2)}) async-start(), calls=%async_computation.12 | async-start | bytes 2621440 | tf_op jit(solution)/shard_map/all_gather | solution.py:241
  13.6 21.3 %copy-start.58 = (u32[32]{0:T(128)S(1)}, u32[32]{0:T(128)}, u32[]{:S(2)}) copy-start(u32[32]{0:T(128)} %constant.166) | copy-start | bytes 388
  13.6 133.0 %all-gather.19.cloned.1.call-start = ((), (), s32[]{:S(2)}) async-start(), calls=%async_computation.9 | async-start | bytes 2359296 | tf_op jit(solution)/shard_map/all_gather | solution.py:238
  15.2 161.6 %all-gather.21.cloned.1.call-start = ((), (), s32[]{:S(2)}) async-start(), calls=%async_computation.10 | async-start | bytes 2359296 | tf_op jit(solution)/shard_map/all_gather | solution.py:238
  17.1 197.8 %reduce-scatter.13.cloned.1.call-start = ((), (), s32[]{:S(2)}) async-start(), calls=%async_computation.15 | async-start | bytes 2359296 | tf_op jit(solution)/shard_map/reduce_scatter | solution.py:305
  33.5 18.1 %copy-start.38 = (f32[1024]{0:T(1024)}, f32[1024]{0:T(1024)S(1)}, u32[]{:S(2)}) copy-start(f32[1024]{0:T(1024)S(1)} %get-tuple-element.107) | copy-start | bytes 12292
  33.5 18.1 %copy-start.40 = (f32[1024]{0:T(1024)}, f32[1024]{0:T(1024)S(1)}, u32[]{:S(2)}) copy-start(f32[1024]{0:T(1024)S(1)} %get-tuple-element.106) | copy-start | bytes 12292
  33.5 18.1 %copy-start.47 = (f32[1024]{0:T(1024)}, f32[1024]{0:T(1024)S(1)}, u32[]{:S(2)}) copy-start(f32[1024]{0:T(1024)S(1)} %get-tuple-element.105) | copy-start | bytes 12292
  120.6 138.9 %all-reduce.4.cloned.1.call-start = ((), (), s32[]{:S(2)}) async-start(), calls=%async_computation.16 | async-start | bytes 524288 | tf_op jit(solution)/shard_map/psum | solution.py:304
  214.9 83.4 %reduce-scatter.15.cloned.1.call-start = ((), (), s32[]{:S(2)}) async-start(), calls=%async_computation.17 | async-start | bytes 2359296 | tf_op jit(solution)/shard_map/reduce_scatter | solution.py:298
  220.9 114.9 %reduce-scatter.17.cloned.1.call-start = ((), (), s32[]{:S(2)}) async-start(), calls=%async_computation.18 | async-start | bytes 2359296 | tf_op jit(solution)/shard_map/reduce_scatter | solution.py:298
  227.1 32.4 %copy-start.14 = (f32[128,1024]{1,0:T(8,128)S(1)}, f32[128,1024]{1,0:T(8,128)}, u32[]{:S(2)}) copy-start(f32[128,1024]{1,0:T(8,128)} %param.22) | copy-start | bytes 1572868
  227.1 32.4 %copy-start.27 = (f32[128,1024]{1,0:T(8,128)S(1)}, f32[128,1024]{1,0:T(8,128)}, u32[]{:S(2)}) copy-start(f32[128,1024]{1,0:T(8,128)} %param.32) | copy-start | bytes 1572868
  227.2 138.4 %all-gather.17.cloned.1.call-start = ((), (), s32[]{:S(2)}) async-start(), calls=%async_computation.8 | async-start | bytes 2359296 | tf_op jit(solution)/shard_map/all_gather | solution.py:238
  262.6 150.9 %all-gather.25.cloned.1.call-start = ((), (), s32[]{:S(2)}) async-start(), calls=%async_computation.19 | async-start | bytes 1310720 | tf_op jit(solution)/shard_map/all_gather | solution.py:299
  298.3 123.9 %all-gather.27.cloned.1.call-start = ((), (), s32[]{:S(2)}) async-start(), calls=%async_computation.20 | async-start | bytes 1310720 | tf_op jit(solution)/shard_map/all_gather | solution.py:299
  335.8 123.7 %reduce-scatter.11.cloned.1.call-start = ((), (), s32[]{:S(2)}) async-start(), calls=%async_computation.14 | async-start | bytes 1769472 | tf_op jit(solution)/shard_map/reduce_scatter | solution.py:298
  387.0 109.3 %reduce-scatter.9.cloned.1.call-start = ((), (), s32[]{:S(2)}) async-start(), calls=%async_computation.13 | async-start | bytes 2621440 | tf_op jit(solution)/shard_map/reduce_scatter | solution.py:259
  396.6 138.4 %reduce-scatter.7.cloned.1.call-start = ((), (), s32[]{:S(2)}) async-start(), calls=%async_computation.11 | async-start | bytes 2621440 | tf_op jit(solution)/shard_map/reduce_scatter | solution.py:258
  419.0 10.8 %copy-start.2 = (f32[128,4096]{1,0:T(8,128)S(1)}, f32[128,4096]{1,0:T(8,128)}, u32[]{:S(2)}) copy-start(f32[128,4096]{1,0:T(8,128)} %param.23) | copy-start | bytes 6291460
  422.2 7.6 %copy-start.11 = (f32[128,4096]{1,0:T(8,128)S(1)}, f32[128,4096]{1,0:T(8,128)}, u32[]{:S(2)}) copy-start(f32[128,4096]{1,0:T(8,128)} %param.33) | copy-start | bytes 6291460
  422.3 7.6 %copy-start.12 = (f32[128,4096]{1,0:T(8,128)S(1)}, f32[128,4096]{1,0:T(8,128)}, u32[]{:S(2)}) copy-start(f32[128,4096]{1,0:T(8,128)} %param.28) | copy-start | bytes 6291460
  485.8 49.2 %copy-start.18 = (bf16[1,256,1024]{2,1,0:T(8,128)(2,1)S(1)}, bf16[1,256,1024]{2,1,0:T(8,128)(2,1)}, u32[]{:S(2)}) copy-start(bf16[1,256,1024]{2,1,0:T(8,128)(2,1)} %param.19) | copy-start | bytes 1572868
  485.8 49.2 %copy-start.45 = (f32[1024]{0:T(1024)S(1)}, f32[1024]{0:T(1024)}, u32[]{:S(2)}) copy-start(f32[1024]{0:T(1024)} %get-tuple-element.102) | copy-start | bytes 12292
  485.8 49.2 %copy-start.46 = (f32[1024]{0:T(1024)S(1)}, f32[1024]{0:T(1024)}, u32[]{:S(2)}) copy-start(f32[1024]{0:T(1024)} %get-tuple-element.103) | copy-start | bytes 12292
  488.9 93.9 %copy-start.37 = (f32[1664]{0:T(1024)S(1)}, f32[1664]{0:T(1024)}, u32[]{:S(2)}) copy-start(f32[1664]{0:T(1024)} %param.25) | copy-start | bytes 19972
  488.9 93.9 %copy-start.54 = (f32[1664]{0:T(1024)S(1)}, f32[1664]{0:T(1024)}, u32[]{:S(2)}) copy-start(f32[1664]{0:T(1024)} %param.35) | copy-start | bytes 19972
  488.9 93.9 %copy-start.55 = (f32[1664]{0:T(1024)S(1)}, f32[1664]{0:T(1024)}, u32[]{:S(2)}) copy-start(f32[1664]{0:T(1024)} %param.30) | copy-start | bytes 19972
  583.5 39.0 %copy-start.42 = (f32[1664]{0:T(1024)}, f32[1664]{0:T(1024)S(1)}, u32[]{:S(2)}) copy-start(f32[1664]{0:T(1024)S(1)} %get-tuple-element.75) | copy-start | bytes 19972
  583.5 39.0 %copy-start.43 = (f32[1664]{0:T(1024)}, f32[1664]{0:T(1024)S(1)}, u32[]{:S(2)}) copy-start(f32[1664]{0:T(1024)S(1)} %get-tuple-element.76) | copy-start | bytes 19972
  (42 other events, 144.3 us)
Sparse Core Ops, SparseCore 0:
  9.9 38.0 all-gather.12
  50.2 27.1 all-gather.14
  79.2 34.4 all-gather.22
  115.7 30.8 all-gather.18
  148.6 28.1 all-gather.20
  179.5 35.2 reduce-scatter.12
  217.8 41.6 all-reduce.3
  262.5 35.7 reduce-scatter.14
  301.3 34.4 reduce-scatter.16
  337.9 27.6 all-gather.16
  367.5 26.1 all-gather.24
  395.5 26.6 all-gather.26
  425.2 34.1 reduce-scatter.10
  463.1 33.1 reduce-scatter.8
  499.7 35.1 reduce-scatter.6
